TPU v7x, 32 devices: a whole 2x2x4 slice. The times are simulated.
32 devices in a mesh: seq: 16 (over z, x, core), fsdp: 2 (over y).
Axes of the slice: x: 2, y: 2, z: 4, core: 2. Of those that a mesh axis runs over, the one named last changes fastest.
Arguments:
- prompt: bfloat16 [2, 256, 4096], P('fsdp'), may hold values from -6 to 6
- lengths: int32 [2], P('fsdp'), may hold values from 1 to 256, 384 in all
- timesteps: int32 [2], P('fsdp'), may hold values from 0 to 999
- ref_errors: float32 [2, 2], P('fsdp'), may hold values from 4.2 to 4.45
- gain_ffn: float32 [4096], replicated, may hold values from 0.5 to 1.5
- w_in_gate: bfloat16 [4096, 8192], P('fsdp', 'seq'), may hold values from -0.09375 to 0.09375
- w_in_up: bfloat16 [4096, 8192], P('fsdp', 'seq'), may hold values from -0.09375 to 0.09375
- w_in_down: bfloat16 [8192, 4096], P('seq', 'fsdp'), may hold values from -0.0625 to 0.0625
- gain_final: float32 [4096], replicated, may hold values from 0.5 to 1.5
- w_context: bfloat16 [4096, 2048], P('fsdp', 'seq'), may hold values from -0.09375 to 0.09375
- image_q: bfloat16 [2, 2, 1024, 1024], P('fsdp', None, 'seq'), may hold values from -128 to 128
- image_k: bfloat16 [2, 2, 1024, 1024], P('fsdp', None, 'seq'), may hold values from -4 to 4
- image_v: bfloat16 [2, 2, 1024, 1024], P('fsdp', None, 'seq'), may hold values from -6 to 6
- w_out: bfloat16 [1024, 1280], P('fsdp'), may hold values from -0.1875 to 0.1875
- target: bfloat16 [2, 2, 1024, 1280], P('fsdp', None, 'seq'), may hold values from -12 to 12
Outputs:
- pair_loss: float32 [2], P('fsdp')
- grad_q: bfloat16 [2, 2, 1024, 1024], P('fsdp', None, None, 'seq')
- grad_k: bfloat16 [2, 2, 1024, 1024], P('fsdp', None, None, 'seq')
- grad_v: bfloat16 [2, 2, 1024, 1024], P('fsdp', None, None, 'seq')
All inputs are finite; a program needn't handle non-finite values. No bound on the sum of `lengths` on one device may be relied on, other than what follows from the above.
Results may differ from a plain program's by a relative error of at most 0.029.
Values may be sent and summed in bfloat16 or wider, within the bound.
No kernel may reach another device: no remote copies, remote signals or barrier semaphores. Data moves between devices by JAX's collectives and lax.ppermute only.
A program may use at most 128 MiB of HBM per device.

v0:
```python
import math
import jax
import jax.numpy as jnp
from jax import lax
from jax.sharding import PartitionSpec as P

PROMPT = 256
HEAD = 64
CH = 1280
dpo_beta = 20.0
norm_eps = 1e-06


def rms_gain(values, gain):
    mean_sq = jnp.mean(values * values, axis=-1, keepdims=True)
    return values * lax.rsqrt(mean_sq + norm_eps) * gain


def noise_level(step_index):
    fraction = (step_index.astype(jnp.float32) + 1.0) / 1000.0
    return 3.0 * fraction / (1.0 + 2.0 * fraction)


def softmax_rows(queries, key_rows, key_mask):
    scores = jnp.einsum("qh,kh->qk", queries, key_rows, preferred_element_type=jnp.float32) * (
        1.0 / math.sqrt(HEAD)
    )
    scores = jnp.where(key_mask[None, :], scores, -jnp.inf)
    top_score = jnp.max(scores, axis=-1, keepdims=True)
    weights = jnp.exp(scores - top_score)
    return (weights / jnp.sum(weights, axis=-1, keepdims=True)).astype(jnp.bfloat16)


def stream_forward(queries, key_rows, value_rows, key_mask):
    seq_len = queries.shape[0]
    block_rows = min(512, seq_len)
    query_blocks = queries.reshape(seq_len // block_rows, block_rows, HEAD)

    def one_block(query_block):
        probs_bf = softmax_rows(query_block, key_rows, key_mask)
        return jnp.dot(probs_bf, value_rows, preferred_element_type=jnp.float32).astype(
            jnp.bfloat16
        )

    return lax.map(one_block, query_blocks).reshape(seq_len, HEAD)


def stream_backward(queries, key_rows, value_rows, key_mask, attended, grad_out):
    seq_len = queries.shape[0]
    block_rows = min(512, seq_len)
    block_count = seq_len // block_rows

    def one_block(carried, pieces):
        key_acc, value_acc = carried
        query_block, out_block, grad_block = pieces
        probs_bf = softmax_rows(query_block, key_rows, key_mask)
        grad_prob = jnp.einsum(
            "qh,kh->qk", grad_block, value_rows, preferred_element_type=jnp.float32
        )
        row_delta = jnp.sum(
            grad_block.astype(jnp.float32) * out_block.astype(jnp.float32), axis=-1, keepdims=True
        )
        grad_score = (
            probs_bf.astype(jnp.float32) * (grad_prob - row_delta) * (1.0 / math.sqrt(HEAD))
        ).astype(jnp.bfloat16)
        grad_query = jnp.dot(grad_score, key_rows, preferred_element_type=jnp.float32).astype(
            jnp.bfloat16
        )
        key_acc = key_acc + jnp.einsum(
            "qk,qh->kh", grad_score[:, :seq_len], query_block, preferred_element_type=jnp.float32
        )
        value_acc = value_acc + jnp.einsum(
            "qk,qh->kh", probs_bf[:, :seq_len], grad_block, preferred_element_type=jnp.float32
        )
        return ((key_acc, value_acc), grad_query)

    zeros_acc = jnp.zeros((seq_len, HEAD), jnp.float32)
    shaped = (
        queries.reshape(block_count, block_rows, HEAD),
        attended.reshape(block_count, block_rows, HEAD),
        grad_out.reshape(block_count, block_rows, HEAD),
    )
    (key_acc, value_acc), grad_query = lax.scan(one_block, (zeros_acc, zeros_acc), shaped)
    return (
        grad_query.reshape(seq_len, HEAD),
        key_acc.astype(jnp.bfloat16),
        value_acc.astype(jnp.bfloat16),
    )


def on_device(
    prompt,
    lengths,
    timesteps,
    ref_errors,
    gain_ffn,
    w_in_gate,
    w_in_up,
    w_in_down,
    gain_final,
    w_context,
    image_q,
    image_k,
    image_v,
    w_out,
    target,
):
    gate_full, up_full, down_full, context_full, out_full = (
        lax.all_gather(w_in_gate, "fsdp", axis=0, tiled=True),
        lax.all_gather(w_in_up, "fsdp", axis=0, tiled=True),
        lax.all_gather(w_in_down, "fsdp", axis=1, tiled=True),
        lax.all_gather(w_context, "fsdp", axis=0, tiled=True),
        lax.all_gather(w_out, "fsdp", axis=0, tiled=True),
    )
    prompt_f32 = prompt[0].astype(jnp.float32)
    normed = rms_gain(prompt_f32, gain_ffn).astype(jnp.bfloat16)
    gate_act = jnp.dot(normed, gate_full, preferred_element_type=jnp.float32)
    up_act = jnp.dot(normed, up_full, preferred_element_type=jnp.float32)
    hidden = (jax.nn.gelu(gate_act, approximate=True) * up_act).astype(jnp.bfloat16)
    partial_value = jnp.dot(hidden, down_full, preferred_element_type=jnp.float32)
    summed = lax.psum(partial_value.astype(jnp.bfloat16), "seq").astype(jnp.float32)
    encoded = rms_gain(prompt_f32 + summed, gain_final).astype(jnp.bfloat16)
    context = jnp.dot(encoded, context_full, preferred_element_type=jnp.float32).astype(
        jnp.bfloat16
    )
    text_keys = context[:, :HEAD]
    text_values = context[:, HEAD:]
    q_heads, k_heads, v_heads = (
        lax.all_to_all(image_q, "seq", split_axis=3, concat_axis=2, tiled=True),
        lax.all_to_all(image_k, "seq", split_axis=3, concat_axis=2, tiled=True),
        lax.all_to_all(image_v, "seq", split_axis=3, concat_axis=2, tiled=True),
    )
    seq_len = q_heads.shape[2]
    key_mask = jnp.arange(seq_len + PROMPT) < seq_len + lengths[0]
    key_sets = []
    value_sets = []
    head_outs = []
    for stream in range(2):
        key_rows = jnp.concatenate([k_heads[0, stream], text_keys], axis=0)
        value_rows = jnp.concatenate([v_heads[0, stream], text_values], axis=0)
        key_sets.append(key_rows)
        value_sets.append(value_rows)
        head_outs.append(stream_forward(q_heads[0, stream], key_rows, value_rows, key_mask))
    attended = jnp.stack(head_outs)[None]
    tok_out = lax.all_to_all(attended, "seq", split_axis=2, concat_axis=3, tiled=True)
    predicted = jnp.einsum("sti,ic->stc", tok_out[0], out_full, preferred_element_type=jnp.float32)
    residual = predicted - target[0].astype(jnp.float32)
    partial_err = jnp.sum(residual * residual, axis=(1, 2))
    error_sums = lax.psum(partial_err, "seq")
    mean_errors = error_sums / (seq_len * CH)
    error_gap = mean_errors[0] - ref_errors[0, 0] - (mean_errors[1] - ref_errors[0, 1])
    sigma_t = noise_level(timesteps[0])
    logit_value = dpo_beta * sigma_t * error_gap
    pair_loss = jax.nn.softplus(logit_value)[None]
    coefficient = sigma_t * jax.nn.sigmoid(logit_value)
    stream_signs = jnp.stack([coefficient, -coefficient])
    grad_pred = (stream_signs[:, None, None] * residual).astype(jnp.bfloat16)
    grad_tok = jnp.einsum(
        "stc,ic->sti", grad_pred, out_full, preferred_element_type=jnp.float32
    ).astype(jnp.bfloat16)
    grad_heads = lax.all_to_all(grad_tok[None], "seq", split_axis=3, concat_axis=2, tiled=True)
    query_grads = []
    key_grads = []
    value_grads = []
    for stream in range(2):
        grad_query, grad_key, grad_value = stream_backward(
            q_heads[0, stream],
            key_sets[stream],
            value_sets[stream],
            key_mask,
            head_outs[stream],
            grad_heads[0, stream],
        )
        query_grads.append(grad_query)
        key_grads.append(grad_key)
        value_grads.append(grad_value)
    return (
        pair_loss,
        jnp.stack(query_grads)[None],
        jnp.stack(key_grads)[None],
        jnp.stack(value_grads)[None],
    )


def solution(mesh):
    return jax.shard_map(
        on_device,
        mesh=mesh,
        in_specs=(
            P("fsdp", None, None),
            P("fsdp"),
            P("fsdp"),
            P("fsdp", None),
            P(),
            P("fsdp", "seq"),
            P("fsdp", "seq"),
            P("seq", "fsdp"),
            P(),
            P("fsdp", "seq"),
            P("fsdp", None, "seq", None),
            P("fsdp", None, "seq", None),
            P("fsdp", None, "seq", None),
            P("fsdp", None),
            P("fsdp", None, "seq", None),
        ),
        out_specs=(
            P("fsdp"),
            P("fsdp", None, None, "seq"),
            P("fsdp", None, None, "seq"),
            P("fsdp", None, None, "seq"),
        ),
        check_vma=False,
    )
```

profile of v0, /device:TPU:0, one launch (start us, length us, event | category | flops | bytes accessed | tf_op | source)
XLA Modules:
  0.0 485.4 jit_solution(12774204976036497098)
XLA Ops:
  10.0 59.0 %all-gather.6.cloned.1.call-done = bf16[4096,512]{1,0:T(8,128)(2,1)} async-done(((bf16[2048,512]{1,0:T(8,128)(2,1)}), bf16[4096,512]{1,0:T(8,128)(2,1)}) %all-gather.6.cloned.1.call-update) | async-done | bytes 4194320 | tf_op jit(solution)/shard_map/all_gather | solution.py:109
  69.0 3.6 fusion.102
  72.6 54.7 %all-gather.10.cloned.1.call-done = bf16[512,4096]{1,0:T(8,128)(2,1)} async-done(((bf16[512,2048]{1,0:T(8,128)(2,1)}), bf16[512,4096]{1,0:T(8,128)(2,1)}) %all-gather.10.cloned.1.call-update) | async-done | bytes 4194320 | tf_op jit(solution)/shard_map/all_gather | solution.py:111
  127.3 58.3 %all-gather.8.cloned.1.call-done = bf16[4096,512]{1,0:T(8,128)(2,1)} async-done(((bf16[2048,512]{1,0:T(8,128)(2,1)}), bf16[4096,512]{1,0:T(8,128)(2,1)}) %all-gather.8.cloned.1.call-update) | async-done | bytes 4194320 | tf_op jit(solution)/shard_map/all_gather | solution.py:110
  185.6 7.3 %convolution_convert_fusion.2 = bf16[256,4096]{1,0:T(8,128)(2,1)} fusion(bf16[512,4096]{1,0:T(8,128)(2,1)} %all-gather.10.cloned.1.call-done, f32[256,512]{1,0:T(8,128)S(1)} %fusion.102, bf16[4096,512]{1,0:T(8,128)(2,1)} %all-gather.8.cloned.1.call-done, bf16[1,256,4096]{2,1,0:T(8,128)(2,1)S(1)} %copy-done.4, f32[4096]{0:T(1024)S(1)} %copy-done.15, ...), kind=kOutput, calls=%fused_computation.97 | convolution fusion | flops 2152988672 | bytes 13124608 | tf_op jit(solution)/shard_map/dot_general | solution.py:120
  195.4 5.6 %all-to-all-start.2 = ((bf16[16,2,4096]{2,1,0:T(2,128)(2,1)}), bf16[16,2,4096]{2,1,0:T(2,128)(2,1)S(1)}, u32[]{:S(2)}, u32[]{:S(2)}) async-start(bf16[16,2,4096]{2,1,0:T(2,128)(2,1)} %reshape.73), calls=%async_computation.2 | async-start | bytes 524288 | tf_op jit(solution)/shard_map/all_to_all | solution.py:131
  202.5 11.2 %all-to-all-done.2 = bf16[16,2,4096]{2,1,0:T(2,128)(2,1)S(1)} async-done(((bf16[16,2,4096]{2,1,0:T(2,128)(2,1)}), bf16[16,2,4096]{2,1,0:T(2,128)(2,1)S(1)}, u32[]{:S(2)}, u32[]{:S(2)}) %all-to-all-start.2) | async-done | bytes 262176 | tf_op jit(solution)/shard_map/all_to_all | solution.py:131
  213.7 3.5 all-to-all-start.1
  219.7 10.4 %all-to-all-done.1 = bf16[16,2,4096]{2,1,0:T(2,128)(2,1)S(1)} async-done(((bf16[16,2,4096]{2,1,0:T(2,128)(2,1)}), bf16[16,2,4096]{2,1,0:T(2,128)(2,1)S(1)}, u32[]{:S(2)}, u32[]{:S(2)}) %all-to-all-start.1) | async-done | bytes 262176 | tf_op jit(solution)/shard_map/all_to_all | solution.py:130
  230.1 4.2 all-to-all-start
  241.4 4.5 all-to-all-done
  249.1 50.5 %all-reduce.2.cloned.1.call-done = bf16[256,4096]{1,0:T(8,128)(2,1)} async-done(((bf16[256,4096]{1,0:T(8,128)(2,1)}), bf16[256,4096]{1,0:T(8,128)(2,1)}) %all-reduce.2.cloned.1.call-update) | async-done | bytes 2097168 | tf_op jit(solution)/shard_map/psum | solution.py:121
  302.0 19.6 %all-gather.12.cloned.1.call-done = bf16[4096,128]{1,0:T(8,128)(2,1)} async-done(((bf16[2048,128]{1,0:T(8,128)(2,1)}), bf16[4096,128]{1,0:T(8,128)(2,1)}) %all-gather.12.cloned.1.call-update) | async-done | bytes 1048592 | tf_op jit(solution)/shard_map/all_gather | solution.py:112
  326.7 6.9 %while.52 = (s32[]{:T(128)}, bf16[2,512,64]{1,2,0:T(8,128)(2,1)}, bf16[2,512,64]{2,1,0:T(8,128)(2,1)}, bf16[1280,64]{1,0:T(8,128)(2,1)S(1)}, bf16[1280,64]{1,0:T(8,128)(2,1)S(1)}, /*index=5*/s32[]{:T(128)}, s32[]{:T(128)}) while((s32[]{:T(128)}, bf16[2,512,64]{1,2,0:T(8,128)(2,1)}, bf16[2,512,64]{2,1,0:T(8,128)(2,1)}, ...), condition=%wide.region_6.7_spmd.clone, body=%wide.region_3.6_spmd.clone.sunk | while | flops 173048064 | bytes 8402513 | solution.py:45
  334.8 3.9 while.53
  340.5 5.6 %all-to-all-start.3 = ((bf16[16,2,4096]{2,1,0:T(2,128)(2,1)}), bf16[16,2,4096]{2,1,0:T(2,128)(2,1)S(1)}, u32[]{:S(2)}, u32[]{:S(2)}) async-start(bf16[16,2,4096]{2,1,0:T(2,128)(2,1)} %reshape.75), calls=%async_computation.3 | async-start | bytes 524288 | tf_op jit(solution)/shard_map/all_to_all | solution.py:145
  347.5 8.7 %all-to-all-done.3 = bf16[16,2,4096]{2,1,0:T(2,128)(2,1)S(1)} async-done(((bf16[16,2,4096]{2,1,0:T(2,128)(2,1)}), bf16[16,2,4096]{2,1,0:T(2,128)(2,1)S(1)}, u32[]{:S(2)}, u32[]{:S(2)}) %all-to-all-start.3) | async-done | bytes 262176 | tf_op jit(solution)/shard_map/all_to_all | solution.py:145
  357.9 4.1 all-gather.14.cloned.1.call-done
  362.0 3.4 multiply_reduce_fusion.1
  365.4 33.0 %psum.15 = f32[2]{0:T(128)S(1)} all-reduce(f32[2]{0:T(128)S(1)} %get-tuple-element.468), channel_id=1, replica_groups=mesh['seq'=16,'fsdp'=2] {'seq'}, use_global_device_ids=true, to_apply=%region_12.13 | all-reduce | flops 2 | bytes 16 | tf_op jit(solution)/shard_map/psum | solution.py:149
  406.8 3.8 all-to-all-start.4
  410.7 9.6 %all-to-all-done.4 = bf16[16,2,4096]{2,1,0:T(2,128)(2,1)S(1)} async-done(((bf16[16,2,4096]{2,1,0:T(2,128)(2,1)}), bf16[16,2,4096]{2,1,0:T(2,128)(2,1)S(1)}, u32[]{:S(2)}, u32[]{:S(2)}) %all-to-all-start.4) | async-done | bytes 262176 | tf_op jit(solution)/shard_map/all_to_all | solution.py:161
  423.6 22.8 %while.54 = (s32[]{:T(128)}, f32[1024,64]{0,1:T(8,128)}, f32[1024,64]{0,1:T(8,128)}, bf16[2,512,64]{1,2,0:T(8,128)(2,1)}, bf16[2,512,64]{2,1,0:T(8,128)(2,1)}, /...) while((s32[]{:T(128)}, f32[1024,64]{0,1:T(8,128)}, ...), condition=%wide.region_17.18_spmd.clone, body=%wide.region_13.17_spmd.clone.sunk | while | flops 394821376 | bytes 17910924 | solution.py:83
  450.4 18.9 %while.55 = (s32[]{:T(128)}, f32[1024,64]{0,1:T(8,128)}, f32[1024,64]{0,1:T(8,128)}, bf16[2,512,64]{1,2,0:T(8,128)(2,1)}, bf16[2,512,64]{2,1,0:T(8,128)(2,1)S(1)...) while((s32[]{:T(128)}, f32[1024,64]{0,1:T(8,128)}, ...), condition=%wide.region_22.23_spmd.clone, body=%wide.region_18.22_spmd.clone.sunk | while | flops 394821376 | bytes 21187588 | solution.py:83
  (183 shorter events, 104.6 us)
Async XLA Ops:
  7.2 2.3 copy-start.4
  7.2 61.8 %all-gather.6.cloned.1.call-start = ((), (), s32[]{:S(2)}) async-start(), calls=%async_computation.5 | async-start | bytes 6291456 | tf_op jit(solution)/shard_map/all_gather | solution.py:109
  7.9 119.4 %all-gather.10.cloned.1.call-start = ((), (), s32[]{:S(2)}) async-start(), calls=%async_computation.7 | async-start | bytes 6291456 | tf_op jit(solution)/shard_map/all_gather | solution.py:111
  8.7 60.4 %copy-start.15 = (f32[4096]{0:T(1024)S(1)}, f32[4096]{0:T(1024)}, u32[]{:S(2)}) copy-start(f32[4096]{0:T(1024)} %param.27) | copy-start | bytes 49156
  8.7 176.9 %all-gather.8.cloned.1.call-start = ((), (), s32[]{:S(2)}) async-start(), calls=%async_computation.6 | async-start | bytes 6291456 | tf_op jit(solution)/shard_map/all_gather | solution.py:110
  9.4 290.2 %all-reduce.2.cloned.1.call-start = ((), (), s32[]{:S(2)}) async-start(), calls=%async_computation.8 | async-start | bytes 4194304 | tf_op jit(solution)/shard_map/psum | solution.py:121
  193.0 8.1 %copy-start.11 = (bf16[1,2,64,1024]{3,2,1,0:T(8,128)(2,1)S(1)}, bf16[1,2,64,1024]{3,2,1,0:T(8,128)(2,1)}, u32[]{:S(2)}) copy-start(bf16[1,2,64,1024]{3,2,1,0:T(8,128)(2,1)} %param.34) | copy-start | bytes 786436
  193.0 128.6 %all-gather.12.cloned.1.call-start = ((), (), s32[]{:S(2)}) async-start(), calls=%async_computation.9 | async-start | bytes 1572864 | tf_op jit(solution)/shard_map/all_gather | solution.py:112
  195.4 18.3 %all-to-all-start.2 = ((bf16[16,2,4096]{2,1,0:T(2,128)(2,1)}), bf16[16,2,4096]{2,1,0:T(2,128)(2,1)S(1)}, u32[]{:S(2)}, u32[]{:S(2)}) async-start(bf16[16,2,4096]{2,1,0:T(2,128)(2,1)} %reshape.73), calls=%async_computation.2 | async-start | bytes 524288 | tf_op jit(solution)/shard_map/all_to_all | solution.py:131
  213.7 16.3 %all-to-all-start.1 = ((bf16[16,2,4096]{2,1,0:T(2,128)(2,1)}), bf16[16,2,4096]{2,1,0:T(2,128)(2,1)S(1)}, u32[]{:S(2)}, u32[]{:S(2)}) async-start(bf16[16,2,4096]{2,1,0:T(2,128)(2,1)} %reshape.71), calls=%async_computation.1 | async-start | bytes 524288 | tf_op jit(solution)/shard_map/all_to_all | solution.py:130
  230.1 5.4 %copy-start.7 = (bf16[16,2,4096]{2,1,0:T(2,128)(2,1)}, bf16[16,2,4096]{2,1,0:T(2,128)(2,1)S(1)}, u32[]{:S(2)}) copy-start(bf16[16,2,4096]{2,1,0:T(2,128)(2,1)S(1)} %all-to-all-done.1) | copy-start | bytes 786436
  230.1 15.9 %all-to-all-start = ((bf16[16,2,4096]{2,1,0:T(2,128)(2,1)}), bf16[16,2,4096]{2,1,0:T(2,128)(2,1)}, u32[]{:S(2)}, u32[]{:S(2)}) async-start(bf16[16,2,4096]{2,1,0:T(2,128)(2,1)} %reshape.69), calls=%async_computation | async-start | bytes 524288 | tf_op jit(solution)/shard_map/all_to_all | solution.py:129
  234.3 127.7 %all-gather.14.cloned.1.call-start = ((), (), s32[]{:S(2)}) async-start(), calls=%async_computation.10 | async-start | bytes 3932160 | tf_op jit(solution)/shard_map/all_gather | solution.py:113
  248.0 73.5 %copy-start.16 = (f32[4096]{0:T(1024)S(1)}, f32[4096]{0:T(1024)}, u32[]{:S(2)}) copy-start(f32[4096]{0:T(1024)} %param.31) | copy-start | bytes 49156
  301.9 22.9 %copy-start.8 = (bf16[1024,64]{1,0:T(8,128)(2,1)S(1)}, bf16[1024,64]{1,0:T(8,128)(2,1)}, u32[]{:S(2)}) copy-start(bf16[1024,64]{1,0:T(8,128)(2,1)} %get-tuple-element.451) | copy-start | bytes 393220
  301.9 22.9 %copy-start.9 = (bf16[1024,64]{1,0:T(8,128)(2,1)S(1)}, bf16[1024,64]{1,0:T(8,128)(2,1)}, u32[]{:S(2)}) copy-start(bf16[1024,64]{1,0:T(8,128)(2,1)} %get-tuple-element.452) | copy-start | bytes 393220
  338.7 19.2 %copy-start.1 = (bf16[1280,64]{1,0:T(8,128)(2,1)}, bf16[1280,64]{1,0:T(8,128)(2,1)S(1)}, u32[]{:S(2)}) copy-start(bf16[1280,64]{1,0:T(8,128)(2,1)S(1)} %get-tuple-element.807) | copy-start | bytes 491524
  338.7 19.2 %copy-start.5 = (bf16[2,512,64]{1,2,0:T(8,128)(2,1)}, bf16[2,512,64]{1,2,0:T(8,128)(2,1)S(1)}, u32[]{:S(2)}) copy-start(bf16[2,512,64]{1,2,0:T(8,128)(2,1)S(1)} %get-tuple-element.734) | copy-start | bytes 393220
  338.7 8.1 %copy-start.14 = (f32[1,2]{1,0:T(1,128)S(1)}, f32[1,2]{1,0:T(1,128)}, u32[]{:S(2)}) copy-start(f32[1,2]{1,0:T(1,128)} %param.26) | copy-start | bytes 28
  340.5 15.6 %all-to-all-start.3 = ((bf16[16,2,4096]{2,1,0:T(2,128)(2,1)}), bf16[16,2,4096]{2,1,0:T(2,128)(2,1)S(1)}, u32[]{:S(2)}, u32[]{:S(2)}) async-start(bf16[16,2,4096]{2,1,0:T(2,128)(2,1)} %reshape.75), calls=%async_computation.3 | async-start | bytes 524288 | tf_op jit(solution)/shard_map/all_to_all | solution.py:145
  362.0 39.7 %copy-start = (bf16[1024,1280]{1,0:T(8,128)(2,1)S(1)}, bf16[1024,1280]{1,0:T(8,128)(2,1)}, u32[]{:S(2)}) copy-start(bf16[1024,1280]{1,0:T(8,128)(2,1)} %all-gather.14.cloned.1.call-done) | copy-start | bytes 7864324
  406.8 13.5 %all-to-all-start.4 = ((bf16[16,2,4096]{2,1,0:T(2,128)(2,1)}), bf16[16,2,4096]{2,1,0:T(2,128)(2,1)S(1)}, u32[]{:S(2)}, u32[]{:S(2)}) async-start(bf16[16,2,4096]{2,1,0:T(2,128)(2,1)} %reshape.77), calls=%async_computation.4 | async-start | bytes 524288 | tf_op jit(solution)/shard_map/all_to_all | solution.py:161
  455.1 2.2 copy-start.12
  464.1 3.2 copy-start.12
  (8 other events, 9.6 us)
Sparse Core Ops, SparseCore 0:
  9.5 59.4 all-gather.5
  70.5 56.7 all-gather.9
  128.9 56.7 all-gather.7
  193.1 106.4 all-reduce.1
  301.0 20.5 all-gather.11
  323.0 38.9 all-gather.13
where the time goes:
time: 487 us; the launch traced here: 485 us
  waiting for transfers between devices  294 us (60%)
  matrix products  57.2 us (12%)
  local copies, waits for them, and re-layouts  36 us (7%)
  blocking collectives  33 us (7%)
  starting transfers between devices  23.1 us (5%)
  other arithmetic  22.4 us (5%)
  between operations  19.8 us (4%)
    all_gather x1, waiting for transfers between devices, on_device(): lax.all_gather(w_in_gate, 'fsdp', axis=0, tiled=True)  59 us
    all_gather x1, waiting for transfers between devices, on_device(): lax.all_gather(w_in_up, 'fsdp', axis=0, tiled=True)  58.3 us
    all_gather x1, waiting for transfers between devices, on_device(): lax.all_gather(w_in_down, 'fsdp', axis=1, tiled=True)  54.7 us
    psum x1, waiting for transfers between devices, on_device(): lax.psum(partial_value.astype(jnp.bfloat16), 'seq').astype(jnp.float32)  50.5 us
    psum x1, blocking collectives, on_device(): error_sums = lax.psum(partial_err, 'seq')  33 us
    all_gather x1, waiting for transfers between devices, on_device(): lax.all_gather(w_context, 'fsdp', axis=0, tiled=True)  19.6 us
    unnamed x43, local copies, waits for them, and re-layouts  16 us
    all_to_all x1, waiting for transfers between devices, on_device(): lax.all_to_all(image_v, 'seq', split_axis=3, concat_axis=2, tiled=True)  11.2 us
  transfers between devices with their start and end apart: 11, of which 11 were waited for; matrix products, arithmetic and copies ran while one was open for 9% of the time, Pallas kernels for 0%

commit v1 on v0

--- a/solution.py
+++ b/solution.py
@@ -9,6 +9,15 @@
 CH = 1280
 dpo_beta = 20.0
 norm_eps = 1e-06
+
+
+def doubling_sum(x, name):
+    size = lax.axis_size(name)
+    total, reach = (x, 1)
+    while reach < size:
+        total = total + lax.ppermute(total, name, [(i, i ^ reach) for i in range(size)])
+        reach = 2 * reach
+    return total
 
 
 def rms_gain(values, gain):
@@ -146,7 +155,7 @@
     predicted = jnp.einsum("sti,ic->stc", tok_out[0], out_full, preferred_element_type=jnp.float32)
     residual = predicted - target[0].astype(jnp.float32)
     partial_err = jnp.sum(residual * residual, axis=(1, 2))
-    error_sums = lax.psum(partial_err, "seq")
+    error_sums = doubling_sum(partial_err, "seq")
     mean_errors = error_sums / (seq_len * CH)
     error_gap = mean_errors[0] - ref_errors[0, 0] - (mean_errors[1] - ref_errors[0, 1])
     sigma_t = noise_level(timesteps[0])

time: 487 us -> 469 us (0.963)
  blocking collectives: 33 us -> 0 us
  waiting for transfers between devices: 294 us -> 303 us
  starting transfers between devices: 23.1 us -> 30.3 us
    psum x1 -> x0, blocking collectives: 33 us -> none  [on_device(): error_sums = lax.psum(partial_err, 'seq')]
    ppermute x0 -> x4, waiting for transfers between devices: none -> 7.4 us  [doubling_sum(): lax.ppermute(total, name, [(i, i ^ reach) for i in range(size)])]
    ppermute x0 -> x4, starting transfers between devices: none -> 5.36 us  [doubling_sum(): lax.ppermute(total, name, [(i, i ^ reach) for i in range(size)])]
    unnamed x43 -> x49, local copies, waits for them, and re-layouts: 16 us -> 15.2 us
  transfers between devices with their start and end apart: 11 -> 15, of which waited for: 11 -> 15; matrix products, arithmetic and copies ran while one was open for 9% -> 9% of each run, Pallas kernels for 0% -> 0%
where the time goes in v1:
time: 469 us; the launch traced here: 467 us
  waiting for transfers between devices  303 us (65%)
  matrix products  57.2 us (12%)
  local copies, waits for them, and re-layouts  35.3 us (8%)
  starting transfers between devices  30.3 us (6%)
  other arithmetic  21.4 us (5%)
  between operations  19.8 us (4%)
    all_gather x1, waiting for transfers between devices, on_device(): lax.all_gather(w_in_gate, 'fsdp', axis=0, tiled=True)  59 us
    all_gather x1, waiting for transfers between devices, on_device(): lax.all_gather(w_in_up, 'fsdp', axis=0, tiled=True)  58.3 us
    all_gather x1, waiting for transfers between devices, on_device(): lax.all_gather(w_in_down, 'fsdp', axis=1, tiled=True)  54.7 us
    psum x1, waiting for transfers between devices, on_device(): lax.psum(partial_value.astype(jnp.bfloat16), 'seq').astype(jnp.float32)  50.5 us
    all_gather x1, waiting for transfers between devices, on_device(): lax.all_gather(w_context, 'fsdp', axis=0, tiled=True)  19.6 us
    unnamed x49, local copies, waits for them, and re-layouts  15.2 us
    all_to_all x1, waiting for transfers between devices, on_device(): lax.all_to_all(image_k, 'seq', split_axis=3, concat_axis=2, tiled=True)  11.3 us
    all_to_all x1, waiting for transfers between devices, on_device(): lax.all_to_all(image_v, 'seq', split_axis=3, concat_axis=2, tiled=True)  11.2 us
  transfers between devices with their start and end apart: 15, of which 15 were waited for; matrix products, arithmetic and copies ran while one was open for 9% of the time, Pallas kernels for 0%

profile of v1, /device:TPU:0, one launch (start us, length us, event | category | flops | bytes accessed | tf_op | source)
XLA Modules:
  0.0 467.3 jit_solution(1488441683863711835)
XLA Ops:
  10.0 59.0 %all-gather.6.cloned.1.call-done = bf16[4096,512]{1,0:T(8,128)(2,1)} async-done(((bf16[2048,512]{1,0:T(8,128)(2,1)}), bf16[4096,512]{1,0:T(8,128)(2,1)}) %all-gather.6.cloned.1.call-update) | async-done | bytes 4194320 | tf_op jit(solution)/shard_map/all_gather | solution.py:118
  69.0 3.6 fusion.102
  72.6 54.7 %all-gather.10.cloned.1.call-done = bf16[512,4096]{1,0:T(8,128)(2,1)} async-done(((bf16[512,2048]{1,0:T(8,128)(2,1)}), bf16[512,4096]{1,0:T(8,128)(2,1)}) %all-gather.10.cloned.1.call-update) | async-done | bytes 4194320 | tf_op jit(solution)/shard_map/all_gather | solution.py:120
  127.3 58.3 %all-gather.8.cloned.1.call-done = bf16[4096,512]{1,0:T(8,128)(2,1)} async-done(((bf16[2048,512]{1,0:T(8,128)(2,1)}), bf16[4096,512]{1,0:T(8,128)(2,1)}) %all-gather.8.cloned.1.call-update) | async-done | bytes 4194320 | tf_op jit(solution)/shard_map/all_gather | solution.py:119
  185.6 7.3 %convolution_convert_fusion.2 = bf16[256,4096]{1,0:T(8,128)(2,1)} fusion(bf16[512,4096]{1,0:T(8,128)(2,1)} %all-gather.10.cloned.1.call-done, f32[256,512]{1,0:T(8,128)S(1)} %fusion.102, bf16[4096,512]{1,0:T(8,128)(2,1)} %all-gather.8.cloned.1.call-done, bf16[1,256,4096]{2,1,0:T(8,128)(2,1)S(1)} %copy-done.4, f32[4096]{0:T(1024)S(1)} %copy-done.18, ...), kind=kOutput, calls=%fused_computation.97 | convolution fusion | flops 2152988672 | bytes 13124608 | tf_op jit(solution)/shard_map/dot_general | solution.py:129
  195.4 5.6 %all-to-all-start.2 = ((bf16[16,2,4096]{2,1,0:T(2,128)(2,1)}), bf16[16,2,4096]{2,1,0:T(2,128)(2,1)S(1)}, u32[]{:S(2)}, u32[]{:S(2)}) async-start(bf16[16,2,4096]{2,1,0:T(2,128)(2,1)} %reshape.73), calls=%async_computation.2 | async-start | bytes 524288 | tf_op jit(solution)/shard_map/all_to_all | solution.py:140
  202.5 11.2 %all-to-all-done.2 = bf16[16,2,4096]{2,1,0:T(2,128)(2,1)S(1)} async-done(((bf16[16,2,4096]{2,1,0:T(2,128)(2,1)}), bf16[16,2,4096]{2,1,0:T(2,128)(2,1)S(1)}, u32[]{:S(2)}, u32[]{:S(2)}) %all-to-all-start.2) | async-done | bytes 262176 | tf_op jit(solution)/shard_map/all_to_all | solution.py:140
  213.7 3.5 all-to-all-start.1
  218.8 11.3 %all-to-all-done.1 = bf16[16,2,4096]{2,1,0:T(2,128)(2,1)S(1)} async-done(((bf16[16,2,4096]{2,1,0:T(2,128)(2,1)}), bf16[16,2,4096]{2,1,0:T(2,128)(2,1)S(1)}, u32[]{:S(2)}, u32[]{:S(2)}) %all-to-all-start.1) | async-done | bytes 262176 | tf_op jit(solution)/shard_map/all_to_all | solution.py:139
  230.1 4.2 all-to-all-start
  241.5 4.5 all-to-all-done
  249.0 50.5 %all-reduce.2.cloned.1.call-done = bf16[256,4096]{1,0:T(8,128)(2,1)} async-done(((bf16[256,4096]{1,0:T(8,128)(2,1)}), bf16[256,4096]{1,0:T(8,128)(2,1)}) %all-reduce.2.cloned.1.call-update) | async-done | bytes 2097168 | tf_op jit(solution)/shard_map/psum | solution.py:130
  302.0 19.6 %all-gather.12.cloned.1.call-done = bf16[4096,128]{1,0:T(8,128)(2,1)} async-done(((bf16[2048,128]{1,0:T(8,128)(2,1)}), bf16[4096,128]{1,0:T(8,128)(2,1)}) %all-gather.12.cloned.1.call-update) | async-done | bytes 1048592 | tf_op jit(solution)/shard_map/all_gather | solution.py:121
  321.5 3.0 fusion.91
  325.8 6.9 %while.52 = (s32[]{:T(128)}, bf16[2,512,64]{1,2,0:T(8,128)(2,1)}, bf16[2,512,64]{2,1,0:T(8,128)(2,1)}, bf16[1280,64]{1,0:T(8,128)(2,1)S(1)}, bf16[1280,64]{1,0:T(8,128)(2,1)S(1)}, /*index=5*/s32[]{:T(128)}, s32[]{:T(128)}) while((s32[]{:T(128)}, bf16[2,512,64]{1,2,0:T(8,128)(2,1)}, bf16[2,512,64]{2,1,0:T(8,128)(2,1)}, ...), condition=%wide.region_6.7_spmd.clone, body=%wide.region_3.6_spmd.clone.sunk | while | flops 173048064 | bytes 8402513 | solution.py:54
  333.9 3.9 while.53
  339.6 5.6 %all-to-all-start.3 = ((bf16[16,2,4096]{2,1,0:T(2,128)(2,1)}), bf16[16,2,4096]{2,1,0:T(2,128)(2,1)S(1)}, u32[]{:S(2)}, u32[]{:S(2)}) async-start(bf16[16,2,4096]{2,1,0:T(2,128)(2,1)} %reshape.75), calls=%async_computation.3 | async-start | bytes 524288 | tf_op jit(solution)/shard_map/all_to_all | solution.py:154
  346.6 8.7 %all-to-all-done.3 = bf16[16,2,4096]{2,1,0:T(2,128)(2,1)S(1)} async-done(((bf16[16,2,4096]{2,1,0:T(2,128)(2,1)}), bf16[16,2,4096]{2,1,0:T(2,128)(2,1)S(1)}, u32[]{:S(2)}, u32[]{:S(2)}) %all-to-all-start.3) | async-done | bytes 262176 | tf_op jit(solution)/shard_map/all_to_all | solution.py:154
  357.0 5.0 %all-gather.14.cloned.1.call-done = bf16[1024,1280]{1,0:T(8,128)(2,1)} async-done(((bf16[512,1280]{1,0:T(8,128)(2,1)}), bf16[1024,1280]{1,0:T(8,128)(2,1)}) %all-gather.14.cloned.1.call-update) | async-done | bytes 2621456 | tf_op jit(solution)/shard_map/all_gather | solution.py:122
  362.0 3.4 multiply_reduce_fusion.1
  386.6 5.6 %all-to-all-start.4 = ((bf16[16,2,4096]{2,1,0:T(2,128)(2,1)}), bf16[16,2,4096]{2,1,0:T(2,128)(2,1)S(1)}, u32[]{:S(2)}, u32[]{:S(2)}) async-start(bf16[16,2,4096]{2,1,0:T(2,128)(2,1)} %reshape.77), calls=%async_computation.4 | async-start | bytes 524288 | tf_op jit(solution)/shard_map/all_to_all | solution.py:170
  392.3 9.9 %all-to-all-done.4 = bf16[16,2,4096]{2,1,0:T(2,128)(2,1)S(1)} async-done(((bf16[16,2,4096]{2,1,0:T(2,128)(2,1)}), bf16[16,2,4096]{2,1,0:T(2,128)(2,1)S(1)}, u32[]{:S(2)}, u32[]{:S(2)}) %all-to-all-start.4) | async-done | bytes 262176 | tf_op jit(solution)/shard_map/all_to_all | solution.py:170
  405.4 22.8 %while.54 = (s32[]{:T(128)}, f32[1024,64]{0,1:T(8,128)}, f32[1024,64]{0,1:T(8,128)}, bf16[2,512,64]{1,2,0:T(8,128)(2,1)}, bf16[2,512,64]{2,1,0:T(8,128)(2,1)}, /...) while((s32[]{:T(128)}, f32[1024,64]{0,1:T(8,128)}, ...), condition=%wide.region_16.17_spmd.clone, body=%wide.region_12.16_spmd.clone.sunk | while | flops 394821376 | bytes 17910924 | solution.py:92
  432.2 18.9 %while.55 = (s32[]{:T(128)}, f32[1024,64]{0,1:T(8,128)}, f32[1024,64]{0,1:T(8,128)}, bf16[2,512,64]{1,2,0:T(8,128)(2,1)}, bf16[2,512,64]{2,1,0:T(8,128)(2,1)S(1)...) while((s32[]{:T(128)}, f32[1024,64]{0,1:T(8,128)}, ...), condition=%wide.region_21.22_spmd.clone, body=%wide.region_17.21_spmd.clone.sunk | while | flops 394821376 | bytes 21187588 | solution.py:92
  (199 shorter events, 112.8 us)
Async XLA Ops:
  7.2 61.8 %all-gather.6.cloned.1.call-start = ((), (), s32[]{:S(2)}) async-start(), calls=%async_computation.5 | async-start | bytes 6291456 | tf_op jit(solution)/shard_map/all_gather | solution.py:118
  7.9 119.4 %all-gather.10.cloned.1.call-start = ((), (), s32[]{:S(2)}) async-start(), calls=%async_computation.7 | async-start | bytes 6291456 | tf_op jit(solution)/shard_map/all_gather | solution.py:120
  8.7 60.4 %copy-start.18 = (f32[4096]{0:T(1024)S(1)}, f32[4096]{0:T(1024)}, u32[]{:S(2)}) copy-start(f32[4096]{0:T(1024)} %param.27) | copy-start | bytes 49156
  8.7 176.9 %all-gather.8.cloned.1.call-start = ((), (), s32[]{:S(2)}) async-start(), calls=%async_computation.6 | async-start | bytes 6291456 | tf_op jit(solution)/shard_map/all_gather | solution.py:119
  9.4 290.1 %all-reduce.2.cloned.1.call-start = ((), (), s32[]{:S(2)}) async-start(), calls=%async_computation.8 | async-start | bytes 4194304 | tf_op jit(solution)/shard_map/psum | solution.py:130
  193.0 24.3 %copy-start.14 = (bf16[1,2,64,1024]{3,2,1,0:T(8,128)(2,1)S(1)}, bf16[1,2,64,1024]{3,2,1,0:T(8,128)(2,1)}, u32[]{:S(2)}) copy-start(bf16[1,2,64,1024]{3,2,1,0:T(8,128)(2,1)} %param.33) | copy-start | bytes 786436
  193.0 128.5 %all-gather.12.cloned.1.call-start = ((), (), s32[]{:S(2)}) async-start(), calls=%async_computation.9 | async-start | bytes 1572864 | tf_op jit(solution)/shard_map/all_gather | solution.py:121
  195.4 18.3 %all-to-all-start.2 = ((bf16[16,2,4096]{2,1,0:T(2,128)(2,1)}), bf16[16,2,4096]{2,1,0:T(2,128)(2,1)S(1)}, u32[]{:S(2)}, u32[]{:S(2)}) async-start(bf16[16,2,4096]{2,1,0:T(2,128)(2,1)} %reshape.73), calls=%async_computation.2 | async-start | bytes 524288 | tf_op jit(solution)/shard_map/all_to_all | solution.py:140
  213.7 16.3 %all-to-all-start.1 = ((bf16[16,2,4096]{2,1,0:T(2,128)(2,1)}), bf16[16,2,4096]{2,1,0:T(2,128)(2,1)S(1)}, u32[]{:S(2)}, u32[]{:S(2)}) async-start(bf16[16,2,4096]{2,1,0:T(2,128)(2,1)} %reshape.71), calls=%async_computation.1 | async-start | bytes 524288 | tf_op jit(solution)/shard_map/all_to_all | solution.py:139
  230.1 15.9 %all-to-all-start = ((bf16[16,2,4096]{2,1,0:T(2,128)(2,1)}), bf16[16,2,4096]{2,1,0:T(2,128)(2,1)}, u32[]{:S(2)}, u32[]{:S(2)}) async-start(bf16[16,2,4096]{2,1,0:T(2,128)(2,1)} %reshape.69), calls=%async_computation | async-start | bytes 524288 | tf_op jit(solution)/shard_map/all_to_all | solution.py:138
  234.3 127.7 %all-gather.14.cloned.1.call-start = ((), (), s32[]{:S(2)}) async-start(), calls=%async_computation.10 | async-start | bytes 3932160 | tf_op jit(solution)/shard_map/all_gather | solution.py:122
  248.0 73.5 %copy-start.19 = (f32[4096]{0:T(1024)S(1)}, f32[4096]{0:T(1024)}, u32[]{:S(2)}) copy-start(f32[4096]{0:T(1024)} %param.31) | copy-start | bytes 49156
  301.9 22.9 %copy-start.8 = (bf16[1024,64]{1,0:T(8,128)(2,1)S(1)}, bf16[1024,64]{1,0:T(8,128)(2,1)}, u32[]{:S(2)}) copy-start(bf16[1024,64]{1,0:T(8,128)(2,1)} %get-tuple-element.450) | copy-start | bytes 393220
  301.9 22.9 %copy-start.9 = (bf16[1024,64]{1,0:T(8,128)(2,1)S(1)}, bf16[1024,64]{1,0:T(8,128)(2,1)}, u32[]{:S(2)}) copy-start(bf16[1024,64]{1,0:T(8,128)(2,1)} %get-tuple-element.451) | copy-start | bytes 393220
  301.9 22.9 %copy-start.10 = (bf16[1024,64]{1,0:T(8,128)(2,1)S(1)}, bf16[1024,64]{1,0:T(8,128)(2,1)}, u32[]{:S(2)}) copy-start(bf16[1024,64]{1,0:T(8,128)(2,1)} %get-tuple-element.452) | copy-start | bytes 393220
  301.9 22.9 %copy-start.11 = (bf16[1024,64]{1,0:T(8,128)(2,1)S(1)}, bf16[1024,64]{1,0:T(8,128)(2,1)}, u32[]{:S(2)}) copy-start(bf16[1024,64]{1,0:T(8,128)(2,1)} %get-tuple-element.453) | copy-start | bytes 393220
  337.8 19.2 %copy-start.1 = (bf16[1280,64]{1,0:T(8,128)(2,1)}, bf16[1280,64]{1,0:T(8,128)(2,1)S(1)}, u32[]{:S(2)}) copy-start(bf16[1280,64]{1,0:T(8,128)(2,1)S(1)} %get-tuple-element.807) | copy-start | bytes 491524
  339.6 15.6 %all-to-all-start.3 = ((bf16[16,2,4096]{2,1,0:T(2,128)(2,1)}), bf16[16,2,4096]{2,1,0:T(2,128)(2,1)S(1)}, u32[]{:S(2)}, u32[]{:S(2)}) async-start(bf16[16,2,4096]{2,1,0:T(2,128)(2,1)} %reshape.75), calls=%async_computation.3 | async-start | bytes 524288 | tf_op jit(solution)/shard_map/all_to_all | solution.py:154
  362.0 19.5 %copy-start = (bf16[1024,1280]{1,0:T(8,128)(2,1)S(1)}, bf16[1024,1280]{1,0:T(8,128)(2,1)}, u32[]{:S(2)}) copy-start(bf16[1024,1280]{1,0:T(8,128)(2,1)} %all-gather.14.cloned.1.call-done) | copy-start | bytes 7864324
  365.3 1.2 collective-permute-start
  366.5 3.6 collective-permute-start.1
  370.1 3.6 collective-permute-start.2
  373.6 4.5 collective-permute-start.3
  386.6 15.6 %all-to-all-start.4 = ((bf16[16,2,4096]{2,1,0:T(2,128)(2,1)}), bf16[16,2,4096]{2,1,0:T(2,128)(2,1)S(1)}, u32[]{:S(2)}, u32[]{:S(2)}) async-start(bf16[16,2,4096]{2,1,0:T(2,128)(2,1)} %reshape.77), calls=%async_computation.4 | async-start | bytes 524288 | tf_op jit(solution)/shard_map/all_to_all | solution.py:170
  (15 other events, 58.1 us)
Sparse Core Ops, SparseCore 0:
  9.5 59.4 all-gather.5
  70.5 56.7 all-gather.9
  128.9 56.7 all-gather.7
  193.1 106.4 all-reduce.1
  300.9 20.5 all-gather.11
  322.9 38.9 all-gather.13
